TPU v7x, 512 devices: a whole 4x8x8 slice. The times are simulated.
512 devices in a mesh: row: 32 (over z, y_hi), col: 16 (over y_lo, x, core).
Axes of the slice: x: 4, y: 8 (y_hi: 4, y_lo: 2; y = y_hi * 2 + y_lo), z: 8, core: 2. Of those that a mesh axis runs over, the one named last changes fastest.
Arguments:
- signal: float32 [32, 65536], P(None, 'row'), may hold values from -8 to 8
- tile_values: bfloat16 [32, 16, 64, 128, 128], P('row', 'col'), may hold values from 1e-12 to 1, as said below
- tile_places: int32 [32, 16, 2, 64], P('row', 'col'), may hold values from 0 to 31, as said below
- tile_counts: int32 [32, 16], P('row', 'col'), may hold values from 16 to 64, as said below
Outputs:
- first_wavelet: float32 [32, 65536], P(None, 'row')
- second_wavelet: float32 [32, 65536], P(None, 'row')
- lowpass: float32 [32, 65536], P(None, 'row')
Inputs may be any that keep to these rules, and one draw needn't show every extreme that they name: `tile_values`: A is symmetric, and every node's row of A has a positive entry on the diagonal. Slots at or after a device's count hold tiles that are not part of A. `tile_places`: place 0 lies below 16, place 1 below 32; the live slots of one device name distinct places. `tile_counts`: some device is full in every draw.
All inputs are finite; a program needn't handle non-finite values.
Results may differ from a plain program's by a relative error of at most 0.0003.
Values may be sent and summed in bfloat16 or wider, within the bound.
No kernel may reach another device: no remote copies, remote signals or barrier semaphores. Data moves between devices by JAX's collectives and lax.ppermute only.
A program may use at most 64 MiB of HBM per device.

v0:
```python
import jax
import jax.numpy as jnp
from jax import lax
from jax.sharding import PartitionSpec as P

highest_precision = lax.Precision.HIGHEST


def broadcast(block, axis, holder):
    block = jnp.where(lax.axis_index(axis) == holder, block, jnp.zeros_like(block))
    return lax.psum(block, axis)


def on_device(signal, tile_values, tile_places, tile_counts):
    channels, row_len = signal.shape
    slot_count = tile_values.shape[2]
    tile_width = tile_values.shape[3]
    tile_rows = row_len // tile_width
    row_size = lax.axis_size("row")
    col_size = lax.axis_size("col")
    halves = row_size // col_size
    blocks = tile_values.reshape(slot_count, tile_width, tile_width)
    places = tile_places.reshape(2, slot_count)
    live_count = tile_counts.reshape(())
    live_slot = (lax.iota(jnp.int32, slot_count) < live_count).astype(jnp.float32)
    row_hot = (places[0][:, None] == lax.iota(jnp.int32, tile_rows)[None, :]).astype(
        jnp.float32
    ) * live_slot[:, None]

    def over_slots(partial_of):
        return partial_of(0, slot_count)

    def degree_part(start, size):
        sums = jnp.sum(blocks, axis=2, dtype=jnp.float32)
        return jnp.einsum("kt,ka->ta", row_hot, sums, precision=highest_precision)

    degree = lax.psum(over_slots(degree_part).reshape(row_len), "col")

    def walk(vector):
        scaled = (vector / degree[None, :]).astype(jnp.bfloat16)
        col_index = lax.axis_index("col")
        pieces = []
        for portion in range(halves):
            pieces.append(broadcast(scaled, "row", col_index * halves + portion))
        column = jnp.concatenate(pieces, axis=1).reshape(channels, halves * tile_rows, tile_width)

        def row_part(start, size):
            picked = jnp.take(column, places[1], axis=1)
            products = jnp.einsum(
                "kab,ckb->cka", blocks, picked, preferred_element_type=jnp.float32
            )
            return jnp.einsum("cka,kt->cta", products, row_hot, precision=highest_precision)

        partial_value = over_slots(row_part)
        spread = lax.psum(partial_value.reshape(channels, row_len), "col")
        return 0.5 * (vector + spread)

    walked = walk(signal)
    lowpass = walk(walked)
    return (jnp.abs(signal - walked), jnp.abs(walked - lowpass), lowpass)


def solution(mesh):
    in_specs = (
        P(None, "row"),
        P("row", "col", None, None, None),
        P("row", "col", None, None),
        P("row", "col"),
    )
    out_specs = (P(None, "row"), P(None, "row"), P(None, "row"))
    return jax.shard_map(
        on_device, mesh=mesh, in_specs=in_specs, out_specs=out_specs, check_vma=False
    )
```

profile of v0, /device:TPU:1, one launch (start us, length us, event | category | flops | bytes accessed | tf_op | source)
XLA Modules:
  0.0 942.9 jit_solution(6482408230794167764)
XLA Ops:
  7.2 0.0 copy-start.3
  7.2 0.0 copy-start.1
  7.2 0.0 all-reduce.13.cloned.1.call-start
  7.9 0.7 slice_bitcast_fusion
  8.6 0.0 copy-start
  8.6 2.4 convert_reduce_fusion
  11.0 0.1 convolution_bitcast_fusion
  11.1 33.8 %psum.49 = f32[2048]{0:T(1024)S(1)} all-reduce(f32[2048]{0:T(1024)S(1)} %convolution_bitcast_fusion), channel_id=1, replica_groups=mesh['row'=32,'col'=16] {'col'}, use_global_device_ids=true, to_apply=%region_1.0 | all-reduce | flops 2048 | bytes 16384 | tf_op jit(solution)/shard_map/psum | solution.py:37
  45.0 0.0 copy-done.1
  45.0 0.7 broadcast_select_fusion.3
  45.7 0.0 all-reduce.13.cloned.1.call-update
  45.7 0.0 all-reduce.7.cloned.1.call-start
  45.8 0.0 copy-done.3
  45.8 293.4 %all-reduce.13.cloned.1.call-done = (bf16[32,2048]{1,0:T(8,128)(2,1)}, bf16[32,2048]{1,0:T(8,128)(2,1)}) async-done(((bf16[32,2048]{1,0:T(8,128)(2,1)}, bf16[32,2048]{1,0:T(8,128)(2,1)}), (bf16[32,2048]{1,0:T(8,128)(2,1)}, bf16[32,2048]{1,0:T(8,128)(2,1)})) %all-reduce.13.cloned.1.call-update) | async-done | bytes 262160 | tf_op jit(solution)/shard_map/psum | solution.py:11
  339.2 1.0 copy_bitcast_fusion.3
  340.2 0.7 gather_fusion
  340.9 0.0 copy-done
  340.9 1.2 fusion.4
  342.1 1.2 fusion.12
  343.3 0.8 copy.24
  344.1 0.0 all-reduce.7.cloned.1.call-update
  344.1 0.0 all-reduce.11.cloned.1.call-start
  344.2 143.4 %all-reduce.7.cloned.1.call-done = f32[32,2048]{1,0:T(8,128)} async-done(((f32[32,2048]{1,0:T(8,128)}), f32[32,2048]{1,0:T(8,128)}) %all-reduce.7.cloned.1.call-update) | async-done | bytes 262160 | tf_op jit(solution)/shard_map/psum | solution.py:55
  487.5 1.7 broadcast_select_fusion.2
  489.2 0.7 broadcast_select_fusion
  489.9 0.0 all-reduce.11.cloned.1.call-update
  489.9 0.0 all-reduce.9.cloned.1.call-start
  489.9 296.2 %all-reduce.11.cloned.1.call-done = (bf16[32,2048]{1,0:T(8,128)(2,1)}, bf16[32,2048]{1,0:T(8,128)(2,1)}) async-done(((bf16[32,2048]{1,0:T(8,128)(2,1)}, bf16[32,2048]{1,0:T(8,128)(2,1)}), (bf16[32,2048]{1,0:T(8,128)(2,1)}, bf16[32,2048]{1,0:T(8,128)(2,1)})) %all-reduce.11.cloned.1.call-update) | async-done | bytes 262160 | tf_op jit(solution)/shard_map/psum | solution.py:11
  786.1 1.0 copy_bitcast_fusion.2
  787.1 0.7 gather_fusion.1
  787.8 0.0 copy-start.2
  787.8 1.2 fusion.7
  789.0 1.2 fusion.10
  790.2 0.8 copy.23
  791.0 0.0 all-reduce.9.cloned.1.call-update
  791.0 143.4 %all-reduce.9.cloned.1.call-done = f32[32,2048]{1,0:T(8,128)} async-done(((f32[32,2048]{1,0:T(8,128)}), f32[32,2048]{1,0:T(8,128)}) %all-reduce.9.cloned.1.call-update) | async-done | bytes 262160 | tf_op jit(solution)/shard_map/psum | solution.py:55
  934.4 0.0 copy-done.2
  934.4 1.9 subtract_abs_fusion
  (3 shorter events, 0.0 us)
Async XLA Ops:
  7.2 38.6 %copy-start.3 = (s32[1,1,2,64]{3,2,1,0:T(2,128)S(1)}, s32[1,1,2,64]{3,2,1,0:T(2,128)}, u32[]{:S(2)}) copy-start(s32[1,1,2,64]{3,2,1,0:T(2,128)} %param.8) | copy-start | bytes 1540
  7.2 37.8 %copy-start.1 = (f32[32,2048]{1,0:T(8,128)S(1)}, f32[32,2048]{1,0:T(8,128)}, u32[]{:S(2)}) copy-start(f32[32,2048]{1,0:T(8,128)} %param.6) | copy-start | bytes 786436
  7.2 332.0 %all-reduce.13.cloned.1.call-start = ((), (), s32[]{:S(2)}) async-start(), calls=%async_computation.3 | async-start | bytes 524288 | tf_op jit(solution)/shard_map/psum | solution.py:11
  8.6 332.3 %copy-start = (bf16[1,1,64,128,128]{4,3,2,1,0:T(8,128)(2,1)S(1)}, bf16[1,1,64,128,128]{4,3,2,1,0:T(8,128)(2,1)}, u32[]{:S(2)}) copy-start(bf16[1,1,64,128,128]{4,3,2,1,0:T(8,128)(2,1)} %param.7) | copy-start | bytes 6291460
  45.7 441.8 %all-reduce.7.cloned.1.call-start = ((), (), s32[]{:S(2)}) async-start(), calls=%async_computation | async-start | bytes 524288 | tf_op jit(solution)/shard_map/psum | solution.py:55
  344.1 442.0 %all-reduce.11.cloned.1.call-start = ((), (), s32[]{:S(2)}) async-start(), calls=%async_computation.2 | async-start | bytes 524288 | tf_op jit(solution)/shard_map/psum | solution.py:11
  489.9 444.5 %all-reduce.9.cloned.1.call-start = ((), (), s32[]{:S(2)}) async-start(), calls=%async_computation.1 | async-start | bytes 524288 | tf_op jit(solution)/shard_map/psum | solution.py:55
  787.8 146.7 %copy-start.2 = (f32[32,2048]{1,0:T(8,128)S(1)}, f32[32,2048]{1,0:T(8,128)}, u32[]{:S(2)}) copy-start(f32[32,2048]{1,0:T(8,128)} %all-reduce.7.cloned.1.call-done) | copy-start | bytes 786436
Sparse Core Ops, SparseCore 0:
  45.9 293.3 all-reduce.12
  344.3 143.2 all-reduce.6
  491.1 294.9 all-reduce.10
  791.1 143.2 all-reduce.8
where the time goes:
time: 943 us
  waiting for transfers between devices  876 us (93%)
  blocking collectives  33.8 us (4%)
  between operations  14.6 us (2%)
    psum x2, waiting for transfers between devices, broadcast(): return lax.psum(block, axis)  590 us
    psum x2, waiting for transfers between devices, walk(): spread = lax.psum(partial_value.reshape(channels, row_len), 'col')  287 us
    psum x1, blocking collectives, on_device(): degree = lax.psum(over_slots(degree_part).reshape(row_len), 'col')  33.8 us
  transfers between devices with their start and end apart: 4, of which 4 were waited for; matrix products, arithmetic and copies ran while one was open for 0% of the time, Pallas kernels for 0%

commit v1 on v0

--- a/solution.py
+++ b/solution.py
@@ -2,6 +2,7 @@
 import jax.numpy as jnp
 from jax import lax
 from jax.sharding import PartitionSpec as P
+from jax.lax import all_gather
 
 highest_precision = lax.Precision.HIGHEST
 
@@ -52,7 +53,8 @@
             return jnp.einsum("cka,kt->cta", products, row_hot, precision=highest_precision)
 
         partial_value = over_slots(row_part)
-        spread = lax.psum(partial_value.reshape(channels, row_len), "col")
+        x_part = partial_value.reshape(channels, row_len)
+        spread = jnp.sum(all_gather(x_part, "col"), axis=0)
         return 0.5 * (vector + spread)
 
     walked = walk(signal)

time: 943 us -> 777 us (0.82)
  waiting for transfers between devices: 876 us -> 707 us
    psum x2 -> x0, waiting for transfers between devices: 287 us -> none  [walk(): spread = lax.psum(partial_value.reshape(channels, row_len), 'col')]
    all_gather x0 -> x2, waiting for transfers between devices: none -> 120 us  [walk(): spread = jnp.sum(all_gather(x_part, 'col'), axis=0)]
where the time goes in v1:
time: 777 us
  waiting for transfers between devices  707 us (91%)
  blocking collectives  33.8 us (4%)
  between operations  14.6 us (2%)
  other arithmetic  12.3 us (2%)
    psum x2, waiting for transfers between devices, broadcast(): return lax.psum(block, axis)  587 us
    all_gather x2, waiting for transfers between devices, walk(): spread = jnp.sum(all_gather(x_part, 'col'), axis=0)  120 us
    psum x1, blocking collectives, on_device(): degree = lax.psum(over_slots(degree_part).reshape(row_len), 'col')  33.8 us
  transfers between devices with their start and end apart: 4, of which 4 were waited for; matrix products, arithmetic and copies ran while one was open for 0% of the time, Pallas kernels for 0%

profile of v1, /device:TPU:1, one launch (start us, length us, event | category | flops | bytes accessed | tf_op | source)
XLA Modules:
  0.0 776.6 jit_solution(13378843212571152486)
XLA Ops:
  7.2 0.0 copy-start.2
  7.2 0.0 copy-start.1
  7.2 0.0 all-reduce.7.cloned.1.call-start
  7.9 0.7 slice_bitcast_fusion
  8.6 0.0 copy-start
  8.6 2.4 convert_reduce_fusion
  11.0 0.1 convolution_bitcast_fusion.2
  11.1 33.8 %psum.35 = f32[2048]{0:T(1024)S(1)} all-reduce(f32[2048]{0:T(1024)S(1)} %convolution_bitcast_fusion.2), channel_id=1, replica_groups=mesh['row'=32,'col'=16] {'col'}, use_global_device_ids=true, to_apply=%region_1.0 | all-reduce | flops 2048 | bytes 16384 | tf_op jit(solution)/shard_map/psum | solution.py:38
  45.0 0.0 copy-done.1
  45.0 0.7 broadcast_select_fusion.3
  45.7 0.0 all-reduce.7.cloned.1.call-update
  45.7 0.0 all-gather.3.cloned.1.call-start
  45.8 0.0 copy-done.2
  45.8 293.4 %all-reduce.7.cloned.1.call-done = (bf16[32,2048]{1,0:T(8,128)(2,1)}, bf16[32,2048]{1,0:T(8,128)(2,1)}) async-done(((bf16[32,2048]{1,0:T(8,128)(2,1)}, bf16[32,2048]{1,0:T(8,128)(2,1)}), (bf16[32,2048]{1,0:T(8,128)(2,1)}, bf16[32,2048]{1,0:T(8,128)(2,1)})) %all-reduce.7.cloned.1.call-update) | async-done | bytes 262160 | tf_op jit(solution)/shard_map/psum | solution.py:12
  339.2 1.0 copy_bitcast_fusion.1
  340.2 0.7 gather_fusion
  340.9 0.0 copy-done
  340.9 1.2 fusion.4
  342.1 1.2 convolution_bitcast_fusion.1
  343.3 0.7 all_gather_reshape.6
  344.1 0.0 all-gather.3.cloned.1.call-update
  344.1 0.0 all-reduce.5.cloned.1.call-start
  344.1 59.9 %all-gather.3.cloned.1.call-done = f32[16,32,2048]{2,1,0:T(8,128)} async-done(((f32[1,32,2048]{2,1,0:T(8,128)}), f32[16,32,2048]{2,1,0:T(8,128)}) %all-gather.3.cloned.1.call-update) | async-done | bytes 4194320 | tf_op jit(solution)/shard_map/all_gather | solution.py:57
  404.0 2.4 reduce_sum.28
  406.5 0.7 broadcast_select_fusion.2
  407.2 0.7 broadcast_select_fusion
  407.8 0.0 all-reduce.5.cloned.1.call-update
  407.9 0.0 all-gather.5.cloned.1.call-start
  407.9 294.0 %all-reduce.5.cloned.1.call-done = (bf16[32,2048]{1,0:T(8,128)(2,1)}, bf16[32,2048]{1,0:T(8,128)(2,1)}) async-done(((bf16[32,2048]{1,0:T(8,128)(2,1)}, bf16[32,2048]{1,0:T(8,128)(2,1)}), (bf16[32,2048]{1,0:T(8,128)(2,1)}, bf16[32,2048]{1,0:T(8,128)(2,1)})) %all-reduce.5.cloned.1.call-update) | async-done | bytes 262160 | tf_op jit(solution)/shard_map/psum | solution.py:12
  701.9 1.0 copy_bitcast_fusion
  702.9 0.7 gather_fusion.1
  703.6 1.2 fusion.7
  704.8 1.2 convolution_bitcast_fusion
  706.0 0.7 all_gather_reshape.7
  706.8 0.0 all-gather.5.cloned.1.call-update
  706.8 59.9 %all-gather.5.cloned.1.call-done = f32[16,32,2048]{2,1,0:T(8,128)} async-done(((f32[1,32,2048]{2,1,0:T(8,128)}), f32[16,32,2048]{2,1,0:T(8,128)}) %all-gather.5.cloned.1.call-update) | async-done | bytes 4194320 | tf_op jit(solution)/shard_map/all_gather | solution.py:57
  766.7 2.4 reduce_sum.29
  769.1 0.9 subtract_abs_fusion
  (3 shorter events, 0.0 us)
Async XLA Ops:
  7.2 38.6 %copy-start.2 = (s32[1,1,2,64]{3,2,1,0:T(2,128)S(1)}, s32[1,1,2,64]{3,2,1,0:T(2,128)}, u32[]{:S(2)}) copy-start(s32[1,1,2,64]{3,2,1,0:T(2,128)} %param.8) | copy-start | bytes 1540
  7.2 37.8 %copy-start.1 = (f32[32,2048]{1,0:T(8,128)S(1)}, f32[32,2048]{1,0:T(8,128)}, u32[]{:S(2)}) copy-start(f32[32,2048]{1,0:T(8,128)} %param.6) | copy-start | bytes 786436
  7.2 332.0 %all-reduce.7.cloned.1.call-start = ((), (), s32[]{:S(2)}) async-start(), calls=%async_computation.3 | async-start | bytes 524288 | tf_op jit(solution)/shard_map/psum | solution.py:12
  8.6 332.3 %copy-start = (bf16[1,1,64,128,128]{4,3,2,1,0:T(8,128)(2,1)S(1)}, bf16[1,1,64,128,128]{4,3,2,1,0:T(8,128)(2,1)}, u32[]{:S(2)}) copy-start(bf16[1,1,64,128,128]{4,3,2,1,0:T(8,128)(2,1)} %param.7) | copy-start | bytes 6291460
  45.7 358.3 %all-gather.3.cloned.1.call-start = ((), (), s32[]{:S(2)}) async-start(), calls=%async_computation | async-start | bytes 4456448 | tf_op jit(solution)/shard_map/all_gather | solution.py:57
  344.1 357.8 %all-reduce.5.cloned.1.call-start = ((), (), s32[]{:S(2)}) async-start(), calls=%async_computation.2 | async-start | bytes 524288 | tf_op jit(solution)/shard_map/psum | solution.py:12
  407.9 358.9 %all-gather.5.cloned.1.call-start = ((), (), s32[]{:S(2)}) async-start(), calls=%async_computation.1 | async-start | bytes 4456448 | tf_op jit(solution)/shard_map/all_gather | solution.py:57
Sparse Core Ops, SparseCore 0:
  45.9 293.3 all-reduce.6
  344.2 59.7 all-gather.2
  408.0 293.8 all-reduce.4
  706.9 59.7 all-gather.4
